TPU v7x, 32 devices: a whole 2x2x4 slice. The times are simulated.
32 devices in a mesh: seq: 4 (over z), head: 8 (over y, x, core).
Axes of the slice: x: 2, y: 2, z: 4, core: 2. Of those that a mesh axis runs over, the one named last changes fastest.
Arguments:
- lengths: int32 [16], replicated, may hold values from 128 to 8192, as said below
- page_owner: int32 [384], replicated, may hold values from 0 to 16, as said below
- page_index: int32 [384], replicated, may hold values from 0 to 127, as said below
- page_dest: int32 [384], replicated, may hold values from 0 to 383, as said below
- src_cache: bfloat16 [384, 8, 64, 256], P(('seq', 'head')), may hold values from -8 to 8
- queries: bfloat16 [2, 16, 4096], replicated, may hold values from -8 to 8
- new_kv: bfloat16 [2, 16, 8, 256], replicated, may hold values from -6 to 6
- hidden_in: bfloat16 [2, 16, 4096], P(None, None, ('seq', 'head')), may hold values from -60 to 60
- out_weight: bfloat16 [4096, 4096], P(None, ('seq', 'head')), may hold values from -1.5 to 1.5
- norm_gain: bfloat16 [4096], P(('seq', 'head')), may hold values from 0.099609375 to 1.8984375
- router: bfloat16 [4096, 8], P(('seq', 'head')), may hold values from -0.09375 to 0.09375
- routes: int32 [2, 16, 2], replicated, may hold values from 0 to 7, all different within a row
- w_gate: bfloat16 [8, 4096, 8192], P('seq', None, 'head'), may hold values from -0.09375 to 0.09375
- w_up: bfloat16 [8, 4096, 8192], P('seq', None, 'head'), may hold values from -0.09375 to 0.09375
- w_down: bfloat16 [8, 8192, 4096], P('seq', 'head'), may hold values from -0.0625 to 0.0625
Outputs:
- page_pool: bfloat16 [8, 384, 64, 256], P('head', 'seq')
- mixed: bfloat16 [2, 16, 4096], P(None, None, ('seq', 'head'))
Inputs may be any that keep to these rules, and one draw needn't show every extreme that they name: Each length is at least 128; one equals 8192; the requests' pages, lengths[r] / 64 rounded up for request r, fit into the 384 pages. `page_owner`: request r owns exactly lengths[r] / 64 rounded up source pages; the other pages carry 16. `page_index`: the pages of request r carry 0 to their count minus 1, each once; pages without request carry 0. `page_dest`: A permutation. Slot g belongs to destination group ((g % 384) // 96) + g // 384. Of the 12 pages that one device holds (pages i * 12 to (i + 1) * 12 - 1), at most 3 go to one group, and every draw has a device that sends exactly 3 to some group.
All inputs are finite; a program needn't handle non-finite values.
Results may differ from a plain program's by a relative error of at most 0.009.
Values may be sent and summed in bfloat16 or wider, within the bound.
No kernel may reach another device: no remote copies, remote signals or barrier semaphores. Data moves between devices by JAX's collectives and lax.ppermute only.
A program may use at most 128 MiB of HBM per device.

v0:
```python
import jax
import jax.numpy as jnp
from jax import lax
from jax.sharding import PartitionSpec as P

D = 4096
HQ = 32
KVH = 8
HD = 128
TOPK = 2
PAGE = 64
REQS = 16


NEG_FILL = -1e30
EPSILON = 1e-05
HIGHEST = lax.Precision.HIGHEST


def joined(array, axis, combine):
    everything = jax.tree.map(lambda part: lax.all_gather(part, axis), array)
    initial = jax.tree.map(lambda part: part[0], everything)

    def hop(k, so_far):
        return combine(so_far, jax.tree.map(lambda part: part[k], everything))

    return lax.fori_loop(1, lax.axis_size(axis), hop, initial)


def gate_mix(logits, picked):
    expert_ids = jnp.arange(logits.shape[1], dtype=jnp.int32)[None, :]
    first_hit = picked[:, 0:1] == expert_ids
    second_hit = picked[:, 1:2] == expert_ids
    first_logit = jnp.sum(jnp.where(first_hit, logits, 0.0), axis=1)
    second_logit = jnp.sum(jnp.where(second_hit, logits, 0.0), axis=1)
    leading = 1.0 / (1.0 + jnp.exp(second_logit - first_logit))
    trailing = 1.0 / (1.0 + jnp.exp(first_logit - second_logit))
    return jnp.where(first_hit, leading[:, None], 0.0) + jnp.where(
        second_hit, trailing[:, None], 0.0
    )


def combine(earlier, later):
    first_top, first_sum, first_acc = earlier
    second_top, second_sum, second_acc = later
    joint_top = jnp.maximum(first_top, second_top)
    first_factor = jnp.exp(first_top - joint_top)
    second_factor = jnp.exp(second_top - joint_top)
    return (
        joint_top,
        first_sum * first_factor + second_sum * second_factor,
        first_acc * first_factor[..., None] + second_acc * second_factor[..., None],
    )


def slot_plan(page_dest, pages_dev, slot_count, slots_dev, replicas, groups):
    part_index = page_dest // slot_count
    within = page_dest % slot_count
    target = within // slots_dev * replicas + part_index
    position = within % slots_dev
    per_device = target.reshape(-1, pages_dev)
    onehot = (per_device[:, :, None] == jnp.arange(groups, dtype=jnp.int32)[None, None, :]).astype(
        jnp.int32
    )
    before = jnp.cumsum(onehot, axis=1) - onehot
    ranking = jnp.sum(before * onehot, axis=2).reshape(-1)
    return (target, position, ranking)


def partial_attention(page_block, owners, page_pos, lengths, grouped, score_scale):
    head_dim = grouped.shape[-1]
    page_len = page_block.shape[2]
    requests = grouped.shape[1]
    clipped = jnp.minimum(owners, requests - 1)
    length_cap = jnp.take(lengths, clipped)
    offsets = page_pos[:, None] * page_len + jnp.arange(page_len, dtype=jnp.int32)[None, :]
    is_live = (owners < requests)[:, None] & (offsets < length_cap[:, None])
    live_mask = is_live[None, :, None, None, :]
    asked_rows = jnp.take(grouped, clipped, axis=1)
    scores = (
        jnp.einsum(
            "spkgd,pktd->spkgt",
            asked_rows,
            page_block[..., :head_dim],
            preferred_element_type=jnp.float32,
        )
        * score_scale
    )
    scores = jnp.where(live_mask, scores, NEG_FILL)
    members = owners[:, None] == jnp.arange(requests, dtype=jnp.int32)[None, :]
    page_top = jnp.max(scores, axis=4)
    row_top = jnp.max(
        jnp.where(members[None, :, :, None, None], page_top[:, :, None], NEG_FILL), axis=1
    )
    weights = jnp.where(
        live_mask, jnp.exp(scores - jnp.take(row_top, clipped, axis=1)[..., None]), 0.0
    )
    member_mask = members.astype(jnp.float32)
    totals = jnp.einsum("pr,spkg->srkg", member_mask, jnp.sum(weights, axis=4), precision=HIGHEST)
    page_out = jnp.einsum(
        "spkgt,pktd->spkgd",
        weights.astype(jnp.bfloat16),
        page_block[..., head_dim:],
        preferred_element_type=jnp.float32,
    )
    weighted = jnp.einsum("pr,spkgd->srkgd", member_mask, page_out, precision=HIGHEST)
    return (row_top, totals, weighted)


def body(
    lengths,
    page_owner,
    page_index,
    page_dest,
    src_cache,
    queries,
    new_kv,
    hidden_in,
    out_weight,
    norm_gain,
    router,
    routes,
    w_gate,
    w_up,
    w_down,
):
    seq_count = lax.axis_size("seq")
    head_count = lax.axis_size("head")
    device_count = seq_count * head_count
    seq_pos = lax.axis_index("seq")
    head_pos = lax.axis_index("head")
    pages_dev = src_cache.shape[0]
    page_total = page_dest.shape[0]
    replicas = head_count // KVH
    groups = seq_count * replicas
    slot_count = page_total // replicas
    slots_dev = pages_dev * KVH
    capacity = (slots_dev + device_count - 1) // device_count
    group_size = HQ // KVH
    step_count = queries.shape[0]
    row_count = step_count * REQS
    source = seq_pos * head_count + head_pos
    target, position, ranking = slot_plan(
        page_dest, pages_dev, slot_count, slots_dev, replicas, groups
    )
    local_target = lax.dynamic_slice_in_dim(target, source * pages_dev, pages_dev)
    local_rank = lax.dynamic_slice_in_dim(ranking, source * pages_dev, pages_dev)
    wanted = jnp.arange(groups * capacity, dtype=jnp.int32)
    matches = (local_target[None, :] == (wanted // capacity)[:, None]) & (
        local_rank[None, :] == (wanted % capacity)[:, None]
    )
    picked_page = jnp.sum(
        jnp.where(matches, jnp.arange(pages_dev, dtype=jnp.int32)[None, :], 0), axis=1
    )
    filled = jnp.any(matches, axis=1)
    packed = jnp.where(
        filled[:, None, None, None],
        jnp.take(src_cache, picked_page, axis=0),
        jnp.zeros((), jnp.bfloat16),
    )
    packed = packed.reshape(seq_count, replicas, capacity, KVH, PAGE, 2 * HD).transpose(
        0, 3, 1, 2, 4, 5
    )
    arrived = lax.all_to_all(
        packed.reshape(device_count, capacity, PAGE, 2 * HD),
        ("seq", "head"),
        split_axis=0,
        concat_axis=0,
        tiled=True,
    )
    arrived = arrived.reshape(device_count * capacity, PAGE, 2 * HD)
    my_group = seq_pos * replicas + head_pos % replicas
    slot_ids = jnp.arange(slots_dev, dtype=jnp.int32)
    holders = (target[None, :] == my_group) & (position[None, :] == slot_ids[:, None])
    flat_index = jnp.arange(page_total, dtype=jnp.int32) // pages_dev * capacity + ranking
    chosen = jnp.sum(jnp.where(holders, flat_index[None, :], 0), axis=1)
    page_pool = jnp.take(arrived, chosen, axis=0)
    grouped = queries.reshape(step_count, REQS, KVH, group_size, HD)
    score_scale = HD ** (-0.5)
    owners = lax.dynamic_slice_in_dim(page_owner, source * pages_dev, pages_dev)
    places = lax.dynamic_slice_in_dim(page_index, source * pages_dev, pages_dev)
    row_top, totals, weighted = partial_attention(
        src_cache, owners, places, lengths, grouped, score_scale
    )
    row_top, totals, weighted = joined(
        (
            row_top.reshape(step_count, REQS, HQ),
            totals.reshape(step_count, REQS, HQ),
            weighted.reshape(step_count, REQS, HQ, HD),
        ),
        ("seq", "head"),
        combine,
    )
    fresh_scores = (
        jnp.einsum(
            "srkgd,urkd->srkgu", grouped, new_kv[..., :HD], preferred_element_type=jnp.float32
        )
        * score_scale
    )
    causal = (jnp.arange(step_count)[:, None] >= jnp.arange(step_count)[None, :])[:, None, None, :]
    fresh_scores = jnp.where(
        causal, fresh_scores.reshape(step_count, REQS, HQ, step_count), NEG_FILL
    )
    joint_top = jnp.maximum(row_top, jnp.max(fresh_scores, axis=3))
    factor = jnp.exp(row_top - joint_top)
    fresh_weights = jnp.where(causal, jnp.exp(fresh_scores - joint_top[..., None]), 0.0)
    totals = totals * factor + jnp.sum(fresh_weights, axis=3)
    fresh_rounded = fresh_weights.reshape(step_count, REQS, KVH, group_size, step_count).astype(
        jnp.bfloat16
    )
    fresh_out = jnp.einsum(
        "srkgu,urkd->srkgd", fresh_rounded, new_kv[..., HD:], preferred_element_type=jnp.float32
    )
    weighted = weighted * factor[..., None] + fresh_out.reshape(step_count, REQS, HQ, HD)
    attended = (weighted / totals[..., None]).reshape(row_count, HQ * HD).astype(jnp.bfloat16)
    attn_out = jnp.dot(attended, out_weight, preferred_element_type=jnp.float32)
    middle = hidden_in.reshape(row_count, -1).astype(jnp.float32) + attn_out
    gain_row = norm_gain.astype(jnp.float32)[None, :]
    squares, routed = lax.psum(
        (
            jnp.sum(middle * middle, axis=1),
            jnp.dot(middle * gain_row, router.astype(jnp.float32), precision=HIGHEST),
        ),
        ("seq", "head"),
    )
    inverse_rms = lax.rsqrt(squares / D + EPSILON)
    logits = routed * inverse_rms[:, None]
    normed = (middle * inverse_rms[:, None] * gain_row).astype(jnp.bfloat16)
    features = lax.all_gather(normed, ("seq", "head"), axis=1, tiled=True)
    mixture = gate_mix(logits, routes.reshape(row_count, TOPK))
    local_experts = w_gate.shape[0]
    local_mix = lax.dynamic_slice_in_dim(mixture, seq_pos * local_experts, local_experts, axis=1)
    gate_act = jnp.einsum("rd,edf->erf", features, w_gate, preferred_element_type=jnp.float32)
    upward = jnp.einsum("rd,edf->erf", features, w_up, preferred_element_type=jnp.float32)
    inner_act = (jax.nn.silu(gate_act) * upward).astype(jnp.bfloat16)
    produced = jnp.einsum("erf,efd->erd", inner_act, w_down, preferred_element_type=jnp.float32)
    moe_out = lax.psum_scatter(
        jnp.sum(local_mix.T[:, :, None] * produced, axis=0).T,
        ("seq", "head"),
        scatter_dimension=0,
        tiled=True,
    )
    mixed = (middle + moe_out.T).astype(jnp.bfloat16).reshape(step_count, REQS, -1)
    return (page_pool[None], mixed)


def solution(mesh):
    in_specs = (
        P(),
        P(),
        P(),
        P(),
        P(("seq", "head"), None, None, None),
        P(),
        P(),
        P(None, None, ("seq", "head")),
        P(None, ("seq", "head")),
        P(("seq", "head")),
        P(("seq", "head"), None),
        P(),
        P("seq", None, "head"),
        P("seq", None, "head"),
        P("seq", "head", None),
    )
    out_specs = (P("head", "seq", None, None), P(None, None, ("seq", "head")))
    return jax.shard_map(body, mesh=mesh, in_specs=in_specs, out_specs=out_specs, check_vma=False)
```

profile of v0, /device:TPU:0, one launch (start us, length us, event | category | flops | bytes accessed | tf_op | source)
XLA Modules:
  0.0 518.8 jit_solution(1423229279083668692)
XLA Ops:
  12.1 2.5 fusion.75
  16.1 2.0 fusion.10
  20.7 4.4 gather_fusion
  25.4 2.3 select_bitcast_fusion
  27.7 2.1 copy.100
  29.8 7.4 %all-to-all-start = ((bf16[32,3,64,256]{3,2,1,0:T(8,128)(2,1)}), bf16[32,3,64,256]{3,2,1,0:T(8,128)(2,1)}, u32[]{:S(2)}, u32[]{:S(2)}) async-start(bf16[32,3,64,256]{3,2,1,0:T(8,128)(2,1)} %bitcast.150), calls=%async_computation | async-start | bytes 6291456 | tf_op jit(solution)/shard_map/all_to_all | solution.py:164
  38.5 2.4 fusion.76
  41.2 115.7 %all_gather.13 = f32[32,2,16,32]{3,2,1,0:T(8,128)S(1)} all-gather(f32[1,2,16,32]{3,2,1,0:T(8,128)S(1)} %copy.112), channel_id=1, replica_groups=mesh['seq'=4,'head'=8] {'seq','head'}, dimensions={0}, use_global_device_ids=true | all-gather | bytes 135168 | tf_op jit(solution)/shard_map/all_gather | solution.py:21
  156.9 68.5 %all_gather.12 = f32[32,2,16,32]{3,2,1,0:T(8,128)S(1)} all-gather(f32[1,2,16,32]{3,2,1,0:T(8,128)S(1)} %copy.106), channel_id=1, replica_groups=mesh['seq'=4,'head'=8] {'seq','head'}, dimensions={0}, use_global_device_ids=true | all-gather | bytes 135168 | tf_op jit(solution)/shard_map/all_gather | solution.py:21
  226.6 49.5 %while.19 = (s32[]{:T(128)}, f32[2,16,32]{2,1,0:T(8,128)S(1)}, f32[2,16,32]{2,1,0:T(8,128)S(1)}, f32[2,16,32,128]{3,2,1,0:T(8,128)S(1)}, f32[32,2,16,32]{3,2,1,0...) while((s32[]{:T(128)}, f32[2,16,32]{2,1,0:T(8,128)S(1)}, ...), condition=%wide.region_9.10_spmd, body=%wide.region_8.9_spmd.sunk | while | flops 399365 | bytes 1613975 | solution.py:27
  226.6 1.5 fusion.87
  228.2 1.5 fusion.87
  229.8 1.5 fusion.87
  231.4 1.5 fusion.87
  233.0 1.5 fusion.87
  234.6 1.5 fusion.87
  236.2 1.5 fusion.87
  237.8 1.5 fusion.87
  239.4 1.5 fusion.87
  241.0 1.5 fusion.87
  242.6 1.5 fusion.87
  244.2 1.5 fusion.87
  245.8 1.5 fusion.87
  247.4 1.5 fusion.87
  249.0 1.5 fusion.87
  250.6 1.5 fusion.87
  252.2 1.5 fusion.87
  253.8 1.5 fusion.87
  255.4 1.5 fusion.87
  257.0 1.5 fusion.87
  258.6 1.5 fusion.87
  260.2 1.5 fusion.87
  261.8 1.5 fusion.87
  263.4 1.5 fusion.87
  265.0 1.5 fusion.87
  266.6 1.5 fusion.87
  268.2 1.5 fusion.87
  269.8 1.5 fusion.87
  271.4 1.5 fusion.87
  273.0 1.5 fusion.87
  279.1 36.9 %all-reduce = (f32[32]{0:T(128)S(1)}, f32[32,8]{0,1:T(8,128)S(1)}) all-reduce(f32[32]{0:T(128)S(1)} %get-tuple-element.237, f32[32,8]{0,1:T(8,128)S(1)} %fusion.48), channel_id=1, replica_groups=mesh['seq'=4,'head'=8] {'seq','head'}, use_global_device_ids=true, to_apply=%region_14.15 | all-reduce | flops 288 | bytes 2304 | tf_op jit(solution)/shard_map/psum | solution.py:219
  316.1 41.0 %all_gather.15 = bf16[32,4096]{1,0:T(8,128)(2,1)S(1)} all-gather(bf16[32,128]{1,0:T(8,128)(2,1)S(1)} %multiply_convert_fusion), channel_id=1, replica_groups=mesh['seq'=4,'head'=8] {'seq','head'}, dimensions={1}, use_global_device_ids=true | all-gather | bytes 270336 | tf_op jit(solution)/shard_map/all_gather | solution.py:229
  357.2 8.9 %convolution_bitcast_fusion.2 = f32[2,32,1024]{2,1,0:T(8,128)S(1)} fusion(bf16[2,4096,1024]{2,1,0:T(8,128)(2,1)} %param.29, bf16[32,4096]{1,0:T(8,128)(2,1)S(1)} %all_gather.15), kind=kOutput, calls=%fused_computation.30 | convolution fusion | flops 536870912 | bytes 17301504 | tf_op jit(solution)/shard_map/rd,edf->erf/dot_general | solution.py:233
  366.1 8.9 %fusion.25 = bf16[2,32,1024]{2,1,0:T(8,128)(2,1)S(1)} fusion(bf16[2,4096,1024]{2,1,0:T(8,128)(2,1)} %param.30, bf16[32,4096]{1,0:T(8,128)(2,1)S(1)} %all_gather.15, f32[2,32,1024]{2,1,0:T(8,128)S(1)} %convolution_bitcast_fusion.2), kind=kOutput, calls=%fused_computation.34 | convolution fusion | flops 537264128 | bytes 17432576 | tf_op jit(solution)/shard_map/rd,edf->erf/dot_general | solution.py:234
  375.1 3.8 fusion.9
  379.0 4.5 gather_fusion.1
  383.6 3.9 bitcast_select_fusion
  387.5 123.2 %reduce-scatter.2.cloned.1.call-done = f32[128,32]{0,1:T(8,128)} async-done(((f32[4096,32]{0,1:T(8,128)}), f32[128,32]{0,1:T(8,128)}) %reduce-scatter.2.cloned.1.call-update) | async-done | bytes 16400 | tf_op jit(solution)/shard_map/reduce_scatter | solution.py:237
  (141 shorter events, 18.6 us)
Async XLA Ops:
  7.2 271.4 %copy-start = (bf16[4096,128]{1,0:T(8,128)(2,1)S(1)}, bf16[4096,128]{1,0:T(8,128)(2,1)}, u32[]{:S(2)}) copy-start(bf16[4096,128]{1,0:T(8,128)(2,1)} %param.25) | copy-start | bytes 3145732
  7.2 218.3 %all-gather.2.cloned.1.call-start = ((), (), s32[]{:S(2)}) async-start(), calls=%async_computation.2 | async-start | bytes 17301504 | tf_op jit(solution)/shard_map/all_gather | solution.py:21
  16.1 3.7 copy-start.4
  29.8 8.7 %copy-start.2 = (bf16[2,16,8,256]{3,2,1,0:T(8,128)(2,1)S(1)}, bf16[2,16,8,256]{3,2,1,0:T(8,128)(2,1)}, u32[]{:S(2)}) copy-start(bf16[2,16,8,256]{3,2,1,0:T(8,128)(2,1)} %param.23) | copy-start | bytes 393220
  29.8 349.2 %all-to-all-start = ((bf16[32,3,64,256]{3,2,1,0:T(8,128)(2,1)}), bf16[32,3,64,256]{3,2,1,0:T(8,128)(2,1)}, u32[]{:S(2)}, u32[]{:S(2)}) async-start(bf16[32,3,64,256]{3,2,1,0:T(8,128)(2,1)} %bitcast.150), calls=%async_computation | async-start | bytes 6291456 | tf_op jit(solution)/shard_map/all_to_all | solution.py:164
  37.2 3.9 copy-start.7
  37.2 3.9 copy-start.6
  37.2 473.4 %reduce-scatter.2.cloned.1.call-start = ((), (), s32[]{:S(2)}) async-start(), calls=%async_computation.3 | async-start | bytes 540672 | tf_op jit(solution)/shard_map/reduce_scatter | solution.py:237
  276.1 2.4 copy-start.3
  277.0 2.0 copy-start.5
  357.2 17.8 %slice-start = ((s8[16777216]{0:T(1024)(128)(4,1)}), s8[4194304]{0:T(1024)(128)(4,1)S(1)}, s32[]{:S(2)}) async-start(s8[16777216]{0:T(1024)(128)(4,1)} %bitcast.148), calls=%async_computation.4 | async-start | bytes 8388608
  357.2 17.8 %slice-start.1 = ((s8[16777216]{0:T(1024)(128)(4,1)}), s8[4194304]{0:T(1024)(128)(4,1)S(1)}, s32[]{:S(2)}) async-start(s8[16777216]{0:T(1024)(128)(4,1)} %bitcast.148), calls=%async_computation.5 | async-start | bytes 8388608
  366.1 9.0 %slice-start.2 = ((s8[16777216]{0:T(1024)(128)(4,1)}), s8[4194304]{0:T(1024)(128)(4,1)S(1)}, s32[]{:S(2)}) async-start(s8[16777216]{0:T(1024)(128)(4,1)} %bitcast.148), calls=%async_computation.6 | async-start | bytes 8388608
  366.1 9.0 %slice-start.3 = ((s8[16777216]{0:T(1024)(128)(4,1)}), s8[4194304]{0:T(1024)(128)(4,1)S(1)}, s32[]{:S(2)}) async-start(s8[16777216]{0:T(1024)(128)(4,1)} %bitcast.148), calls=%async_computation.7 | async-start | bytes 8388608
  379.0 132.9 %copy-start.1 = (bf16[4096,128]{1,0:T(8,128)(2,1)S(1)}, bf16[4096,128]{1,0:T(8,128)(2,1)}, u32[]{:S(2)}) copy-start(bf16[4096,128]{1,0:T(8,128)(2,1)} %param.25) | copy-start | bytes 3145732
Sparse Core Ops, SparseCore 0:
  19.9 166.8 all-gather.1
  379.0 131.6 reduce-scatter.1
where the time goes:
time: 521 us; the launch traced here: 519 us
  blocking collectives  262 us (50%)
  waiting for transfers between devices  123 us (24%)
  other arithmetic  60.5 us (12%)
  matrix products  30.4 us (6%)
  local copies, waits for them, and re-layouts  19.7 us (4%)
  between operations  14.5 us (3%)
  starting transfers between devices  7.51 us (1%)
    all_gather x2, blocking collectives, joined(): everything = jax.tree.map(lambda part: lax.all_gather(part, axis), array)  184 us
    reduce_scatter x1, waiting for transfers between devices, body(): lax.psum_scatter(jnp.sum(local_mix.T[:, :, None] * produced, axis=0).T, (...  123 us
    add x31, other arithmetic, combine(): first_acc * first_factor[..., None] + second_acc * second_factor[..., None]  47.9 us
    all_gather x1, blocking collectives, body(): features = lax.all_gather(normed, ('seq', 'head'), axis=1, tiled=True)  41 us
    psum x1, blocking collectives, body(): lax.psum((jnp.sum(middle * middle, axis=1), jnp.dot(middle * gain_row, ro...  36.9 us
  transfers between devices with their start and end apart: 3, of which 1 were waited for; matrix products, arithmetic and copies ran while one was open for 19% of the time, Pallas kernels for 0%

commit v1 on v0

v1 whole, which is shorter than its diff:
```python
import functools

import jax
import jax.numpy as jnp
from jax import lax
from jax.experimental import pallas as pl
from jax.experimental.pallas import tpu as pltpu
from jax.sharding import PartitionSpec as P

D = 4096
HQ = 32
KVH = 8
HD = 128
TOPK = 2
PAGE = 64
REQS = 16
LANES = 128
STAT = 16

NEG_FILL = -1e30
EPSILON = 1e-05
HIGHEST = lax.Precision.HIGHEST
VMEM_SPEC = pl.BlockSpec(memory_space=pltpu.VMEM)


def shift_perm(count, shift):
    return [(i, (i + shift) % count) for i in range(count)]


def pieces(value):
    hi = value.astype(jnp.bfloat16).astype(jnp.float32)
    rest = value - hi
    mid = rest.astype(jnp.bfloat16).astype(jnp.float32)
    return hi, mid, rest - mid


def eye_mask(rows):
    return lax.broadcasted_iota(jnp.int32, (rows, LANES), 0) == lax.broadcasted_iota(
        jnp.int32, (rows, LANES), 1
    )


def to_lanes(column):
    rows = column.shape[0]
    return jnp.sum(
        jnp.where(eye_mask(rows), jnp.broadcast_to(column, (rows, LANES)), 0.0),
        axis=0,
        keepdims=True,
    )


def to_column(row, rows):
    return jnp.sum(
        jnp.where(eye_mask(rows), jnp.broadcast_to(row, (rows, LANES)), 0.0), axis=1, keepdims=True
    )


def stat_block(row):
    hi, mid, low = pieces(row)
    index = lax.broadcasted_iota(jnp.int32, (STAT, LANES), 0)
    block = jnp.where(index == 0, hi, jnp.where(index == 1, mid, jnp.where(index == 2, low, 0.0)))
    return block.astype(jnp.bfloat16)


def pack_kernel(picked_ref, page_ref, out_ref):
    out_ref[...] = jnp.swapaxes(page_ref[...], 0, 1)


def pack_pages(picked, src_cache):
    count = picked.shape[0]
    heads, page_len, width = src_cache.shape[1:]
    return pl.pallas_call(
        pack_kernel,
        out_shape=jax.ShapeDtypeStruct((heads, count, page_len, width), src_cache.dtype),
        grid_spec=pltpu.PrefetchScalarGridSpec(
            num_scalar_prefetch=1,
            grid=(count,),
            in_specs=[
                pl.BlockSpec((1, heads, page_len, width), lambda i, picked_ref: (picked_ref[i], 0, 0, 0))
            ],
            out_specs=pl.BlockSpec((heads, 1, page_len, width), lambda i, picked_ref: (0, i, 0, 0)),
        ),
        cost_estimate=pl.CostEstimate(
            flops=0, transcendentals=0, bytes_accessed=2 * count * heads * page_len * width * 2
        ),
    )(picked, src_cache)


def place_kernel(aliased, shift, seq_count, spots_ref, pages_ref, *rest):
    out_ref, sems = rest[-2], rest[-1]
    count = pages_ref.shape[0]
    me = lax.axis_index("seq")
    base = lax.rem(me - shift + seq_count, seq_count) * count

    def copy(i):
        spot = spots_ref[base + i]
        return spot >= 0, pltpu.make_async_copy(
            pages_ref.at[i], out_ref.at[jnp.maximum(spot, 0)], sems.at[i]
        )

    for i in range(count):
        there, move = copy(i)

        @pl.when(there)
        def _():
            move.start()

    for i in range(count):
        there, move = copy(i)

        @pl.when(there)
        def _():
            move.wait()


def place_pages(spots, pages, pool, slots_dev, shift, seq_count):
    count = pages.shape[0]
    aliased = pool is not None
    args = (spots, pages) + ((pool,) if aliased else ())
    return pl.pallas_call(
        functools.partial(place_kernel, aliased, shift, seq_count),
        out_shape=jax.ShapeDtypeStruct((slots_dev,) + pages.shape[1:], pages.dtype),
        in_specs=[pl.BlockSpec(memory_space=pltpu.SMEM), VMEM_SPEC]
        + ([pl.BlockSpec(memory_space=pl.ANY)] if aliased else []),
        out_specs=pl.BlockSpec(memory_space=pl.ANY),
        scratch_shapes=[pltpu.SemaphoreType.DMA((count,))],
        input_output_aliases={2: 0} if aliased else {},
    )(*args)


def attend_kernel(
    group,
    devices,
    where_ref,
    owner_ref,
    index_ref,
    length_ref,
    query_ref,
    fresh_ref,
    pages_ref,
    out_ref,
    top_ref,
    sum_ref,
    acc_ref,
):
    step = pl.program_id(0)
    requests, rows, head_dim = query_ref.shape
    heads, page_len = pages_ref.shape[1:3]
    per_head = rows // heads
    scale = head_dim ** (-0.5)
    source = where_ref[0]

    @pl.when(step == 0)
    def _():
        top_ref[...] = jnp.full_like(top_ref, NEG_FILL)
        sum_ref[...] = jnp.zeros_like(sum_ref)
        acc_ref[...] = jnp.zeros_like(acc_ref)

    def partial(request, keys, values, mask):
        scores = (
            lax.dot_general(
                query_ref[request], keys, (((1,), (1,)), ((), ())), preferred_element_type=jnp.float32
            )
            * scale
        )
        scores = jnp.where(mask, scores, NEG_FILL)
        top = jnp.max(scores, axis=1, keepdims=True)
        weights = jnp.where(mask, jnp.exp(scores - top), 0.0)
        total = jnp.sum(weights, axis=1, keepdims=True)
        out = jnp.dot(weights.astype(jnp.bfloat16), values, preferred_element_type=jnp.float32)
        return top, total, out

    def merge(request, part):
        top, total, out = part
        old = top_ref[request]
        top = jnp.broadcast_to(top, old.shape)
        new = jnp.maximum(old, top)
        keep = jnp.exp(old - new)
        gain = jnp.exp(top - new)
        top_ref[request] = new
        sum_ref[request] = sum_ref[request] * keep + gain * total
        acc_ref[request] = acc_ref[request] * keep + gain * out

    columns = heads * page_len
    row_head = lax.broadcasted_iota(jnp.int32, (rows, columns), 0) // per_head
    column = lax.broadcasted_iota(jnp.int32, (rows, columns), 1)
    same_head = row_head == column // page_len
    token = column % page_len
    parts = []
    for i in range(group):
        page = source * (group * pl.num_programs(0)) + step * group + i
        owner = owner_ref[page]
        request = jnp.minimum(owner, requests - 1)
        alive = jnp.where(
            owner < requests, length_ref[request] - index_ref[page] * page_len, 0
        )
        keys = pages_ref[i, :, :, :head_dim].reshape(columns, head_dim)
        values = pages_ref[i, :, :, head_dim:].reshape(columns, head_dim)
        parts.append((request, partial(request, keys, values, same_head & (token < alive))))
    for request, part in parts:
        merge(request, part)

    @pl.when(step == pl.num_programs(0) - 1)
    def _():
        head_count = out_ref.shape[0]
        block = rows // head_count
        fresh_rows = fresh_ref.shape[1]
        steps = fresh_rows // heads
        row = lax.broadcasted_iota(jnp.int32, (rows, fresh_rows), 0)
        col = lax.broadcasted_iota(jnp.int32, (rows, fresh_rows), 1)
        row_step = (row % block) // (block // steps)
        mask = (row // per_head == col % heads) & (col // heads <= row_step)
        for extra in range((requests + devices - 1) // devices):
            request = source + extra * devices

            @pl.when(request < requests)
            def _():
                keys = fresh_ref[request, :, :head_dim]
                values = fresh_ref[request, :, head_dim:]
                merge(request, partial(request, keys, values, mask))

        span = requests * block
        for dest in range(head_count):
            part = pl.ds(dest * block, block)
            total = sum_ref[:, part, :].reshape(span, LANES)
            top = top_ref[:, part, :].reshape(span, LANES)
            acc = acc_ref[:, part, :].reshape(span, LANES)
            some = total > 0.0
            safe = jnp.where(some, total, 1.0)
            out_ref[dest, :span, :] = (acc / safe).astype(jnp.bfloat16)
            joint = jnp.where(some, top + jnp.log(safe), NEG_FILL)
            row_vec = jnp.sum(jnp.where(eye_mask(span), joint, 0.0), axis=0, keepdims=True)
            out_ref[dest, span:, :] = stat_block(row_vec)


def partial_attention(source, owner, index, lengths, query, fresh, pages, head_count, devices):
    requests, rows, head_dim = query.shape
    page_count, heads, page_len, width = pages.shape
    group = max(g for g in (1, 2, 3, 4) if page_count % g == 0)
    span = requests * rows // head_count
    whole = lambda shape: pl.BlockSpec(shape, lambda i, *refs: (0,) * len(shape))
    return pl.pallas_call(
        functools.partial(attend_kernel, group, devices),
        out_shape=jax.ShapeDtypeStruct((head_count, span + STAT, LANES), jnp.bfloat16),
        grid_spec=pltpu.PrefetchScalarGridSpec(
            num_scalar_prefetch=4,
            grid=(page_count // group,),
            in_specs=[
                whole(query.shape),
                whole(fresh.shape),
                pl.BlockSpec((group, heads, page_len, width), lambda i, *refs: (i, 0, 0, 0)),
            ],
            out_specs=whole((head_count, span + STAT, LANES)),
            scratch_shapes=[pltpu.VMEM((requests, rows, LANES), jnp.float32)] * 3,
        ),
        cost_estimate=pl.CostEstimate(
            flops=4 * page_count * rows * heads * page_len * head_dim,
            transcendentals=page_count * rows * heads * page_len,
            bytes_accessed=2 * page_count * heads * page_len * width,
        ),
    )(source, owner, index, lengths, query, fresh, pages)


def mix_partials(blocks, span):
    rows = []
    for block in blocks:
        stats = block[span:, :].astype(jnp.float32)
        rows.append(stats[0:1] + stats[1:2] + stats[2:3])
    top = functools.reduce(jnp.maximum, rows)
    weights = [jnp.exp(row - top) for row in rows]
    total = sum(weights)
    out = 0.0
    for block, weight in zip(blocks, weights):
        out = out + to_column(weight / total, span) * block[:span, :].astype(jnp.float32)
    return out, top + jnp.log(total)


def gather_partials_kernel(parts_ref, out_ref):
    count, size, _ = parts_ref.shape
    span = size - STAT
    out, joint = mix_partials([parts_ref[i] for i in range(count)], span)
    out_ref[:span, :] = out.astype(jnp.bfloat16)
    out_ref[span:, :] = stat_block(joint)


def gather_partials(parts):
    return pl.pallas_call(
        gather_partials_kernel,
        out_shape=jax.ShapeDtypeStruct(parts.shape[1:], parts.dtype),
        in_specs=[VMEM_SPEC],
        out_specs=VMEM_SPEC,
    )(parts)


def finish_attention_kernel(steps, *refs):
    out_ref, flat_ref = refs[-2:]
    blocks = [ref[...] for ref in refs[:-2]]
    span = blocks[0].shape[0] - STAT
    out, _ = mix_partials(blocks, span)
    flat_ref[...] = out
    block = span // REQS
    per_step = block // steps
    for s in range(steps):
        for a in range(per_step):
            out_ref[s * REQS : (s + 1) * REQS, a * HD : (a + 1) * HD] = flat_ref[
                pl.ds(s * per_step + a, REQS, stride=block), :
            ].astype(jnp.bfloat16)


def finish_attention(blocks, steps):
    span = blocks[0].shape[0] - STAT
    per_step = span // REQS // steps
    return pl.pallas_call(
        functools.partial(finish_attention_kernel, steps),
        out_shape=jax.ShapeDtypeStruct((steps * REQS, per_step * HD), jnp.bfloat16),
        in_specs=[VMEM_SPEC] * len(blocks),
        out_specs=VMEM_SPEC,
        scratch_shapes=[pltpu.VMEM((span, LANES), jnp.float32)],
    )(*blocks)


def project_kernel(att_ref, weight_ref, hidden_ref, gain_ref, router_ref, middle_ref, out_ref):
    heads, rows, depth = att_ref.shape
    total = jnp.zeros(middle_ref.shape, jnp.float32)
    for h in range(heads):
        total = total + jnp.dot(
            att_ref[h], weight_ref[h * depth : (h + 1) * depth, :], preferred_element_type=jnp.float32
        )
    middle = hidden_ref[...].astype(jnp.float32) + total
    middle_ref[...] = middle
    scaled = middle * gain_ref[...].astype(jnp.float32)
    width = middle.shape[1]
    if width < LANES:
        out_ref[:rows, :] = jnp.zeros((rows, LANES), jnp.bfloat16)
    out_ref[:rows, :width] = scaled.astype(jnp.bfloat16)
    squares = jnp.sum(middle * middle, axis=1, keepdims=True)
    routed = jnp.dot(
        scaled,
        router_ref[...].astype(jnp.float32),
        precision=HIGHEST,
        preferred_element_type=jnp.float32,
    )
    lane = lax.broadcasted_iota(jnp.int32, (rows, LANES), 1)
    stats = jnp.where(lane == 8, squares, routed)
    out_ref[rows:, :] = spread_stats(stats)


def spread_stats(stats):
    hi, mid, low = pieces(stats)
    return (hi + pltpu.roll(mid, 16, 1) + pltpu.roll(low, 32, 1)).astype(jnp.bfloat16)


def joined_stats(block):
    wide = block.astype(jnp.float32)
    lane = lax.broadcasted_iota(jnp.int32, wide.shape, 1)
    total = wide + pltpu.roll(wide, LANES - 16, 1) + pltpu.roll(wide, LANES - 32, 1)
    return jnp.where(lane < 16, total, 0.0)


def project(att, weight, hidden, gain, router):
    rows, width = hidden.shape
    return pl.pallas_call(
        project_kernel,
        out_shape=(
            jax.ShapeDtypeStruct((rows, width), jnp.float32),
            jax.ShapeDtypeStruct((2 * rows, LANES), jnp.bfloat16),
        ),
        in_specs=[VMEM_SPEC] * 5,
        out_specs=(VMEM_SPEC, VMEM_SPEC),
    )(att, weight, hidden, gain, router)


def stack_kernel(*refs):
    out_ref = refs[-1]
    parts = refs[:-1]
    count = len(parts)
    rows = parts[0].shape[0] // 2
    me = lax.axis_index("seq")
    stats = 0.0
    for shift, ref in enumerate(parts):
        origin = lax.rem(me - shift + count, count)
        out_ref[origin] = ref[:rows, :]
        stats = stats + joined_stats(ref[rows:, :])
    out_ref[count] = spread_stats(stats)


def stack_parts(parts):
    rows = parts[0].shape[0] // 2
    return pl.pallas_call(
        stack_kernel,
        out_shape=jax.ShapeDtypeStruct((len(parts) + 1, rows, LANES), jnp.bfloat16),
        in_specs=[VMEM_SPEC] * len(parts),
        out_specs=VMEM_SPEC,
    )(*parts)


def features_kernel(local_experts, all_ref, routes_ref, feat_ref, aux_ref):
    heads, blocks, rows, _ = all_ref.shape
    seqs = blocks - 1
    width = feat_ref.shape[1] // (seqs * heads)
    for h in range(heads):
        for s in range(seqs):
            at = (s * heads + h) * width
            feat_ref[:, at : at + width] = all_ref[h, s, :, :width]
    stats = 0.0
    for h in range(heads):
        stats = stats + joined_stats(all_ref[h, seqs])
    lane = lax.broadcasted_iota(jnp.int32, (rows, LANES), 1)
    squares = jnp.sum(jnp.where(lane == 8, stats, 0.0), axis=1, keepdims=True)
    inverse = lax.rsqrt(squares / feat_ref.shape[1] + EPSILON)
    logits = stats * inverse
    first = routes_ref[:, 0:1] == lane
    second = routes_ref[:, 1:2] == lane
    first_logit = jnp.sum(jnp.where(first, logits, 0.0), axis=1, keepdims=True)
    second_logit = jnp.sum(jnp.where(second, logits, 0.0), axis=1, keepdims=True)
    leading = 1.0 / (1.0 + jnp.exp(second_logit - first_logit))
    trailing = 1.0 / (1.0 + jnp.exp(first_logit - second_logit))
    mixture = jnp.where(first, leading, 0.0) + jnp.where(second, trailing, 0.0)
    base = lax.axis_index("seq") * local_experts
    aux = jnp.where(lane == 0, inverse, 0.0)
    for e in range(local_experts):
        share = jnp.sum(jnp.where(lane == base + e, mixture, 0.0), axis=1, keepdims=True)
        aux = jnp.where(lane == 1 + e, share, aux)
    aux_ref[...] = aux


def features_of(everything, routes, local_experts, width):
    heads, blocks, rows, _ = everything.shape
    return pl.pallas_call(
        functools.partial(features_kernel, local_experts),
        out_shape=(
            jax.ShapeDtypeStruct((rows, heads * (blocks - 1) * width), jnp.bfloat16),
            jax.ShapeDtypeStruct((rows, LANES), jnp.float32),
        ),
        in_specs=[VMEM_SPEC] * 2,
        out_specs=(VMEM_SPEC, VMEM_SPEC),
    )(everything, routes)


def spread(block, axis):
    count = lax.axis_size(axis)
    return lax.all_to_all(
        jnp.broadcast_to(block[None], (count,) + block.shape), axis, 0, 0, tiled=True
    )


def body(
    lengths,
    page_owner,
    page_index,
    page_dest,
    src_cache,
    queries,
    new_kv,
    hidden_in,
    out_weight,
    norm_gain,
    router,
    routes,
    w_gate,
    w_up,
    w_down,
):
    seq_count = lax.axis_size("seq")
    head_count = lax.axis_size("head")
    device_count = seq_count * head_count
    seq_pos = lax.axis_index("seq")
    head_pos = lax.axis_index("head")
    pages_dev = src_cache.shape[0]
    page_total = page_dest.shape[0]
    replicas = head_count // KVH
    slot_count = page_total // replicas
    slots_dev = pages_dev * KVH
    capacity = (slots_dev + device_count - 1) // device_count
    step_count = queries.shape[0]
    row_count = step_count * REQS
    heads_dev = HQ // head_count
    source = seq_pos * head_count + head_pos

    part_index = page_dest // slot_count
    within = page_dest % slot_count
    target_seq = within // slots_dev
    position = within % slots_dev
    before = jnp.arange(pages_dev)[:, None] > jnp.arange(pages_dev)[None, :]
    local_part = lax.dynamic_slice_in_dim(part_index, source * pages_dev, pages_dev)
    local_seq = lax.dynamic_slice_in_dim(target_seq, source * pages_dev, pages_dev)
    bin_of = (local_seq + seq_count - seq_pos) % seq_count * replicas + local_part
    rank = jnp.sum(((bin_of[:, None] == bin_of[None, :]) & before).astype(jnp.int32), axis=1)
    wanted = jnp.arange(seq_count * replicas * capacity, dtype=jnp.int32)
    picked = jnp.sum(
        jnp.where(
            (bin_of * capacity + rank)[None, :] == wanted[:, None],
            jnp.arange(pages_dev, dtype=jnp.int32)[None, :],
            0,
        ),
        axis=1,
    )
    mine = ((target_seq == seq_pos) & (part_index == head_pos % replicas)).reshape(-1, pages_dev)
    mine_rank = jnp.sum((mine[:, None, :] & before[None]).astype(jnp.int32), axis=2)
    spots = jnp.sum(
        jnp.where(
            mine[:, None, :]
            & (mine_rank[:, None, :] == jnp.arange(capacity, dtype=jnp.int32)[None, :, None]),
            position.reshape(-1, pages_dev)[:, None, :] + 1,
            0,
        ),
        axis=2,
    )
    spots = spots.reshape(-1) - 1

    bin_size = replicas * capacity
    moved = []
    for shift in range(seq_count):
        packed = pack_pages(picked[shift * bin_size : (shift + 1) * bin_size], src_cache)
        packed = packed.reshape(head_count, capacity, PAGE, 2 * HD)
        if shift:
            packed = lax.ppermute(packed, "seq", shift_perm(seq_count, shift))
        moved.append(packed)

    query = (
        queries.reshape(step_count, REQS, head_count, heads_dev, HD)
        .transpose(1, 2, 0, 3, 4)
        .reshape(REQS, step_count * HQ, HD)
    )
    fresh = new_kv.transpose(1, 0, 2, 3).reshape(REQS, step_count * KVH, 2 * HD)
    parts = partial_attention(
        jnp.reshape(source, (1,)),
        page_owner,
        page_index,
        lengths,
        query,
        fresh,
        src_cache,
        head_count,
        device_count,
    )
    parts = lax.all_to_all(parts, "head", 0, 0, tiled=True)
    part = gather_partials(parts)
    blocks = [part] + [
        lax.ppermute(part, "seq", shift_perm(seq_count, shift)) for shift in range(1, seq_count)
    ]
    attended = finish_attention(blocks, step_count)
    attended = spread(attended, "head").reshape(head_count, row_count, heads_dev * HD)

    middle, payload = project(
        attended,
        out_weight,
        hidden_in.reshape(row_count, -1),
        norm_gain.reshape(1, -1),
        jnp.pad(router, ((0, 0), (0, LANES - router.shape[1]))),
    )
    payloads = [payload] + [
        lax.ppermute(payload, "seq", shift_perm(seq_count, shift)) for shift in range(1, seq_count)
    ]
    stacked = stack_parts(payloads)
    everything = spread(stacked, "head").reshape((head_count,) + stacked.shape)
    local_experts = w_gate.shape[0]
    features, aux = features_of(everything, routes.reshape(row_count, TOPK), local_experts, hidden_in.shape[2])
    inverse = aux[:, 0:1]
    gate_act = jnp.einsum("rd,edf->erf", features, w_gate, preferred_element_type=jnp.float32)
    upward = jnp.einsum("rd,edf->erf", features, w_up, preferred_element_type=jnp.float32)
    inner_act = (jax.nn.silu(gate_act * inverse) * (upward * inverse)).astype(jnp.bfloat16)
    produced = jnp.einsum("erf,efd->erd", inner_act, w_down, preferred_element_type=jnp.float32)
    local_mix = aux[:, 1 : 1 + local_experts]
    terms = jnp.sum(local_mix.T[:, :, None] * produced, axis=0).astype(jnp.bfloat16)
    terms = terms.reshape(row_count, seq_count, head_count, -1).transpose(2, 1, 0, 3)
    terms = lax.all_to_all(terms, "head", 0, 0, tiled=True)
    plane = jnp.sum(terms.astype(jnp.float32), axis=0)
    moe_out = lax.dynamic_index_in_dim(plane, seq_pos, 0, keepdims=False)
    plane = plane.astype(jnp.bfloat16)
    for shift in range(1, seq_count):
        share = lax.dynamic_index_in_dim(plane, (seq_pos + shift) % seq_count, 0, keepdims=False)
        moe_out = moe_out + lax.ppermute(share, "seq", shift_perm(seq_count, shift)).astype(
            jnp.float32
        )
    mixed = (middle + moe_out).astype(jnp.bfloat16).reshape(step_count, REQS, -1)

    pool = None
    for shift in range(seq_count):
        arrived = lax.all_to_all(moved[shift], "head", 0, 0, tiled=True)
        arrived = arrived.reshape(head_count * capacity, PAGE, 2 * HD)
        pool = place_pages(spots, arrived, pool, slots_dev, shift, seq_count)
    return (pool[None], mixed)


def solution(mesh):
    in_specs = (
        P(),
        P(),
        P(),
        P(),
        P(("seq", "head"), None, None, None),
        P(),
        P(),
        P(None, None, ("seq", "head")),
        P(None, ("seq", "head")),
        P(("seq", "head")),
        P(("seq", "head"), None),
        P(),
        P("seq", None, "head"),
        P("seq", None, "head"),
        P("seq", "head", None),
    )
    out_specs = (P("head", "seq", None, None), P(None, None, ("seq", "head")))
    return jax.shard_map(body, mesh=mesh, in_specs=in_specs, out_specs=out_specs, check_vma=False)
```

time: 521 us -> 212 us (0.41)
  blocking collectives: 262 us -> 12.6 us
  waiting for transfers between devices: 123 us -> 48 us
  other arithmetic: 60.5 us -> 5.22 us
  starting transfers between devices: 7.51 us -> 62.6 us
  Pallas kernels: 0 us -> 39.6 us
  between operations: 14.5 us -> 0.97 us
  matrix products: 30.4 us -> 20.9 us
    all_gather x3 -> x0, blocking collectives: 225 us -> none  [the longest x2 184 us: joined(): everything = jax.tree.map(lambda part: lax.all_gather(part, axis), array)]
    reduce_scatter x1 -> x0, waiting for transfers between devices: 123 us -> none  [body(): lax.psum_scatter(jnp.sum(local_mix.T[:, :, None] * produced, axis=0).T, (...]
    add x64 -> x3, other arithmetic: 48.6 us -> 0.69 us  [the longest x1 0.6 us: body(): position.reshape(-1, pages_dev)[:, None, :] + 1]
    pallas_call x0 -> x14, Pallas kernels: none -> 39.6 us  [the longest x4 14.3 us: pack_pages(): pl.pallas_call(pack_kernel, out_shape=jax.ShapeDtypeStruct((heads, count,...]
    psum x1 -> x0, blocking collectives: 36.9 us -> none  [body(): lax.psum((jnp.sum(middle * middle, axis=1), jnp.dot(middle * gain_row, ro...]
    ppermute x0 -> x12, starting transfers between devices: none -> 36.1 us  [the longest x3 19.8 us: body(): lax.ppermute(share, 'seq', shift_perm(seq_count, shift)).astype(jnp.float32)]
    ppermute x0 -> x12, waiting for transfers between devices: none -> 35.5 us  [the longest x3 24.7 us: body(): packed = lax.ppermute(packed, 'seq', shift_perm(seq_count, shift))]
    all_to_all x1 -> x7, starting transfers between devices: 7.43 us -> 26.4 us  [the longest x4 15.4 us: body(): arrived = lax.all_to_all(moved[shift], 'head', 0, 0, tiled=True)]
  transfers between devices with their start and end apart: 3 -> 19, of which waited for: 1 -> 11; matrix products, arithmetic and copies ran while one was open for 19% -> 17% of each run, Pallas kernels for 0% -> 11%
where the time goes in v1:
time: 212 us; the launch traced here: 210 us
  starting transfers between devices  62.6 us (30%)
  waiting for transfers between devices  48 us (23%)
  Pallas kernels  39.6 us (19%)
  matrix products  20.9 us (10%)
  local copies, waits for them, and re-layouts  20 us (9%)
  blocking collectives  12.6 us (6%)
  other arithmetic  5.22 us (2%)
    ppermute x3, waiting for transfers between devices, body(): packed = lax.ppermute(packed, 'seq', shift_perm(seq_count, shift))  24.7 us
    ppermute x3, starting transfers between devices, body(): lax.ppermute(share, 'seq', shift_perm(seq_count, shift)).astype(jnp.float32)  19.8 us
    all_to_all x4, starting transfers between devices, body(): arrived = lax.all_to_all(moved[shift], 'head', 0, 0, tiled=True)  15.4 us
    pallas_call x4, Pallas kernels, pack_pages(): pl.pallas_call(pack_kernel, out_shape=jax.ShapeDtypeStruct((heads, count,...  14.3 us
    all_to_all x1, blocking collectives, body(): parts = lax.all_to_all(parts, 'head', 0, 0, tiled=True)  12.6 us
    dot_general x1, matrix products, body(): jnp.einsum('rd,edf->erf', features, w_gate, preferred_element_type=jnp.fl...  8.98 us
    pallas_call x4, Pallas kernels, place_pages(): pl.pallas_call(functools.partial(place_kernel, aliased, shift, seq_count)...  8.93 us
    dot_general x1, matrix products, body(): jnp.einsum('rd,edf->erf', features, w_up, preferred_element_type=jnp.floa...  8.92 us
  transfers between devices with their start and end apart: 19, of which 11 were waited for; matrix products, arithmetic and copies ran while one was open for 17% of the time, Pallas kernels for 11%

profile of v1, /device:TPU:0, one launch (start us, length us, event | category | flops | bytes accessed | tf_op | source)
XLA Modules:
  0.0 209.9 jit_solution(7127228001817370572)
XLA Ops:
  0.7 1.2 reshape.81
  3.3 6.9 %shard_map.166 = bf16[8,144,128]{2,1,0:T(8,128)(2,1)} custom-call(s32[1]{0:T(128)} %bitcast.5.where_ref, s32[384]{0:T(512)} %owner_ref.1, s32[384]{0:T(512)} %index_ref.1, s32[16]{0:T(128)} %length_ref.1, bf16[16,64,128]{2,1,0:T(8,128)(2,1)} %bitcast.62, bf16[16,16,256]{2,1,0:T(8,128)(2,1)} %copy_bitcast_fusion.fresh_ref, bf16[12,8,64,256]{3,2,1,0:T(8,128)(2,1)} %pages_ref.1), custom_call_target="tpu_custom_call" | custom-call | flops 201326592 | bytes 3145728 | tf_op jit(solution)/shard_map/pallas_call | solution.py:242
  10.2 12.6 %all_to_all.40.parts_ref = bf16[8,144,128]{2,1,0:T(8,128)(2,1)} all-to-all(bf16[8,144,128]{2,1,0:T(8,128)(2,1)} %shard_map.166), channel_id=1, replica_groups=mesh['seq'=4,'head'=8] {'head'}, dimensions={0} | all-to-all | bytes 589824 | tf_op jit(solution)/shard_map/all_to_all | solution.py:537
  22.8 1.8 shard_map.167.refs_0_
  24.6 1.8 collective-permute-start.3
  26.4 2.3 %collective-permute-start.4 = (bf16[144,128]{1,0:T(8,128)(2,1)}, bf16[144,128]{1,0:T(8,128)(2,1)S(1)}, u32[]{:S(2)}, u32[]{:S(2)}) collective-permute-start(bf16[144,128]{1,0:T(8,128)(2,1)} %shard_map.167.refs_0_), channel_id=1, source_target_pairs={{0,16},{8,24},{16,0},{24,8},{1,17},{9,25},{17,1},{25,9},{2,18},{10... | collective-permute-start | bytes 110600 | tf_op jit(solution)/shard_map/ppermute | solution.py:540
  28.6 1.3 collective-permute-start.5
  30.7 1.1 collective-permute-done.4.refs_2_
  31.7 1.1 collective-permute-done.5.refs_3_
  33.4 1.6 shard_map.168
  35.1 1.5 broadcast_in_dim.32
  36.5 3.4 %all-to-all-start.5 = ((bf16[8,32,512]{2,1,0:T(8,128)(2,1)}), bf16[8,32,512]{2,1,0:T(8,128)(2,1)S(1)}, u32[]{:S(2)}, u32[]{:S(2)}) async-start(bf16[8,32,512]{2,1,0:T(8,128)(2,1)} %broadcast_in_dim.32), calls=%async_computation.5 | async-start | bytes 524288 | tf_op jit(solution)/shard_map/all_to_all | solution.py:442
  42.4 4.4 %all-to-all-done.5.att_ref = bf16[8,32,512]{2,1,0:T(8,128)(2,1)S(1)} async-done(((bf16[8,32,512]{2,1,0:T(8,128)(2,1)}), bf16[8,32,512]{2,1,0:T(8,128)(2,1)S(1)}, u32[]{:S(2)}, u32[]{:S(2)}) %all-to-all-start.5) | async-done | bytes 262176 | tf_op jit(solution)/shard_map/all_to_all | solution.py:442
  47.5 2.4 %shard_map.169 = (f32[32,128]{1,0:T(8,128)}, bf16[64,128]{1,0:T(8,128)(2,1)}) custom-call(bf16[8,32,512]{2,1,0:T(8,128)(2,1)} %copy-done.8, bf16[4096,128]{1,0:T(8,128)(2,1)} %weight_ref.1, bf16[32,128]{1,0:T(8,128)(2,1)} %bitcast.66, bf16[1,128]{1,0:T(2,128)(2,1)} %bitcast.71, bf16[128,128]{1,0:T(8,128)(2,1)} %pad.4.router_ref), custom_call_target="tpu_custom_call" | custom-call | tf_op jit(solution)/shard_map/pallas_call | solution.py:362
  50.4 3.2 %collective-permute-start.7 = (bf16[64,128]{1,0:T(8,128)(2,1)}, bf16[64,128]{1,0:T(8,128)(2,1)S(1)}, u32[]{:S(2)}, u32[]{:S(2)}) collective-permute-start(bf16[64,128]{1,0:T(8,128)(2,1)} %get-tuple-element.7.refs_0_), channel_id=1, source_target_pairs={{0,16},{8,24},{16,0},{24,8},{1,17},{9,25},{17,1},{25,9},{2,18},{10... | collective-permute-start | bytes 49160 | tf_op jit(solution)/shard_map/ppermute | solution.py:553
  54.5 1.3 collective-permute-done.6.refs_1_
  55.8 1.8 collective-permute-done.8.refs_3_
  58.2 1.6 shard_map.170
  59.8 1.5 broadcast_in_dim.33
  61.3 3.4 %all-to-all-start.6 = ((bf16[8,5,32,128]{3,2,1,0:T(8,128)(2,1)}), bf16[8,5,32,128]{3,2,1,0:T(8,128)(2,1)S(1)}, u32[]{:S(2)}, u32[]{:S(2)}) async-start(bf16[8,5,32,128]{3,2,1,0:T(8,128)(2,1)} %broadcast_in_dim.33), calls=%async_computation.6 | async-start | bytes 655360 | tf_op jit(solution)/shard_map/all_to_all | solution.py:442
  65.5 3.5 %shard_map.160 = bf16[8,3,64,256]{3,2,1,0:T(8,128)(2,1)} custom-call(s32[3]{0:T(128)} %get-tuple-element.17.picked_ref, bf16[12,8,64,256]{3,2,1,0:T(8,128)(2,1)} %pages_ref.1), custom_call_target="tpu_custom_call" | custom-call | bytes 1572864 | tf_op jit(solution)/shard_map/pallas_call | solution.py:72
  69.7 1.4 copy.70
  71.1 3.6 %shard_map.161 = bf16[8,3,64,256]{3,2,1,0:T(8,128)(2,1)} custom-call(s32[3]{0:T(128)} %get-tuple-element.16.picked_ref, bf16[12,8,64,256]{3,2,1,0:T(8,128)(2,1)} %pages_ref.1), custom_call_target="tpu_custom_call" | custom-call | bytes 1572864 | tf_op jit(solution)/shard_map/pallas_call | solution.py:72
  74.6 4.1 %all-to-all-start.3 = ((bf16[8,3,64,256]{3,2,1,0:T(8,128)(2,1)}), bf16[8,3,64,256]{3,2,1,0:T(8,128)(2,1)S(1)}, u32[]{:S(2)}, u32[]{:S(2)}) async-start(bf16[8,3,64,256]{3,2,1,0:T(8,128)(2,1)} %shard_map.161), calls=%async_computation.3 | async-start | bytes 1572864 | tf_op jit(solution)/shard_map/all_to_all | solution.py:580
  78.8 2.0 shard_map.171
  82.6 9.0 %fusion.2 = f32[2,32,1024]{2,1,0:T(8,128)S(1)} fusion(bf16[2,4096,1024]{2,1,0:T(8,128)(2,1)} %param.27, bf16[32,4096]{1,0:T(8,128)(2,1)} %get-tuple-element.9, f32[32]{0:T(128)S(1)} %slice_reduce_fusion), kind=kOutput, calls=%fused_computation.5 | convolution fusion | flops 536936448 | bytes 17301632 | tf_op jit(solution)/shard_map/rd,edf->erf/dot_general | solution.py:560
  91.6 8.9 %fusion.4 = bf16[2,32,1024]{2,1,0:T(8,128)(2,1)S(1)} fusion(bf16[2,4096,1024]{2,1,0:T(8,128)(2,1)} %param.28, bf16[32,4096]{1,0:T(8,128)(2,1)S(1)} %copy-done.6, f32[2,32,1024]{2,1,0:T(8,128)S(1)} %fusion.2, f32[32]{0:T(128)S(1)} %slice_reduce_fusion), kind=kOutput, calls=%fused_computation.7 | convolution fusion | flops 537329664 | bytes 17432704 | tf_op jit(solution)/shard_map/rd,edf->erf/dot_general | solution.py:561
  100.6 3.0 %fusion = bf16[32,4096]{1,0:T(8,128)(2,1)S(1)} fusion(bf16[2,32,1024]{2,1,0:T(8,128)(2,1)S(1)} %fusion.4, bf16[2,1024,4096]{2,1,0:T(8,128)(2,1)S(1)} %bitcast.56, f32[2,32]{1,0:T(2,128)S(1)} %copy.68), kind=kOutput, calls=%fused_computation.1 | convolution fusion | flops 537264128 | bytes 17170688 | tf_op jit(solution)/shard_map/erf,efd->erd/dot_general | solution.py:563
  104.5 4.2 %all-to-all-start.7 = ((bf16[8,4,32,128]{3,1,2,0:T(4,128)(2,1)}), bf16[8,4,32,128]{3,1,2,0:T(4,128)(2,1)S(1)}, u32[]{:S(2)}, u32[]{:S(2)}) async-start(bf16[8,4,32,128]{3,1,2,0:T(4,128)(2,1)} %copy.69), calls=%async_computation.7 | async-start | bytes 524288 | tf_op jit(solution)/shard_map/all_to_all | solution.py:567
  108.7 3.6 %shard_map.159 = bf16[8,3,64,256]{3,2,1,0:T(8,128)(2,1)} custom-call(s32[3]{0:T(128)} %get-tuple-element.18.picked_ref, bf16[12,8,64,256]{3,2,1,0:T(8,128)(2,1)} %pages_ref.1), custom_call_target="tpu_custom_call" | custom-call | bytes 1572864 | tf_op jit(solution)/shard_map/pallas_call | solution.py:72
  112.2 2.5 %collective-permute-start.1 = (bf16[8,3,64,256]{3,2,1,0:T(8,128)(2,1)}, bf16[8,3,64,256]{3,2,1,0:T(8,128)(2,1)S(1)}, u32[]{:S(2)}, u32[]{:S(2)}) collective-permute-start(bf16[8,3,64,256]{3,2,1,0:T(8,128)(2,1)} %shard_map.159), channel_id=1, source_target_pairs={{0,16},{8,24},{16,0},{24,8},{1,17},{9,25},{17,1},{25,9},{2,18},{10... | collective-permute-start | bytes 2359304 | tf_op jit(solution)/shard_map/ppermute | solution.py:517
  115.6 3.5 %all-to-all-start.2 = ((bf16[8,3,64,256]{3,2,1,0:T(8,128)(2,1)}), bf16[8,3,64,256]{3,2,1,0:T(8,128)(2,1)S(1)}, u32[]{:S(2)}, u32[]{:S(2)}) async-start(bf16[8,3,64,256]{3,2,1,0:T(8,128)(2,1)} %collective-permute-done.2), calls=%async_computation.2 | async-start | bytes 1572864 | tf_op jit(solution)/shard_map/all_to_all | solution.py:580
  119.1 3.7 %shard_map.158 = bf16[8,3,64,256]{3,2,1,0:T(8,128)(2,1)} custom-call(s32[3]{0:T(128)} %get-tuple-element.19.picked_ref, bf16[12,8,64,256]{3,2,1,0:T(8,128)(2,1)} %pages_ref.1), custom_call_target="tpu_custom_call" | custom-call | bytes 1572864 | tf_op jit(solution)/shard_map/pallas_call | solution.py:72
  122.8 3.1 %collective-permute-start = (bf16[8,3,64,256]{3,2,1,0:T(8,128)(2,1)}, bf16[8,3,64,256]{3,2,1,0:T(8,128)(2,1)S(1)}, u32[]{:S(2)}, u32[]{:S(2)}) collective-permute-start(bf16[8,3,64,256]{3,2,1,0:T(8,128)(2,1)} %shard_map.158), channel_id=1, source_target_pairs={{0,24},{8,0},{16,8},{24,16},{1,25},{9,1},{17,9},{25,17},{2,26},{10... | collective-permute-start | bytes 2359304 | tf_op jit(solution)/shard_map/ppermute | solution.py:517
  125.9 24.7 %collective-permute-done.1 = bf16[8,3,64,256]{3,2,1,0:T(8,128)(2,1)S(1)} collective-permute-done((bf16[8,3,64,256]{3,2,1,0:T(8,128)(2,1)}, bf16[8,3,64,256]{3,2,1,0:T(8,128)(2,1)S(1)}, u32[]{:S(2)}, u32[]{:S(2)}) %collective-permute-start.1) | collective-permute-done | bytes 786464 | tf_op jit(solution)/shard_map/ppermute | solution.py:517
  150.6 0.9 copy-done.10
  151.5 4.2 %all-to-all-start.1 = ((bf16[8,3,64,256]{3,2,1,0:T(8,128)(2,1)}), bf16[8,3,64,256]{3,2,1,0:T(8,128)(2,1)S(1)}, u32[]{:S(2)}, u32[]{:S(2)}) async-start(bf16[8,3,64,256]{3,2,1,0:T(8,128)(2,1)} %copy-done.10), calls=%async_computation.1 | async-start | bytes 1572864 | tf_op jit(solution)/shard_map/all_to_all | solution.py:580
  160.1 0.9 copy-done.9
  161.0 7.3 %all-to-all-done.1 = bf16[8,3,64,256]{3,2,1,0:T(8,128)(2,1)S(1)} async-done(((bf16[8,3,64,256]{3,2,1,0:T(8,128)(2,1)}), bf16[8,3,64,256]{3,2,1,0:T(8,128)(2,1)S(1)}, u32[]{:S(2)}, u32[]{:S(2)}) %all-to-all-start.1) | async-done | bytes 786464 | tf_op jit(solution)/shard_map/all_to_all | solution.py:580
  168.3 3.5 %all-to-all-start = ((bf16[8,3,64,256]{3,2,1,0:T(8,128)(2,1)}), bf16[8,3,64,256]{3,2,1,0:T(8,128)(2,1)S(1)}, u32[]{:S(2)}, u32[]{:S(2)}) async-start(bf16[8,3,64,256]{3,2,1,0:T(8,128)(2,1)} %copy-done.9), calls=%async_computation | async-start | bytes 1572864 | tf_op jit(solution)/shard_map/all_to_all | solution.py:580
  173.8 2.2 %shard_map.162.rest_0_ = bf16[96,64,256]{2,1,0:T(8,128)(2,1)} custom-call(s32[96]{0:T(128)} %sub.25.spots_ref, bf16[24,64,256]{2,1,0:T(8,128)(2,1)} %bitcast.60), custom_call_target="tpu_custom_call" | custom-call | tf_op jit(solution)/shard_map/pallas_call | solution.py:120
  176.3 19.2 %collective-permute-start.11 = (bf16[32,128]{1,0:T(8,128)(2,1)S(1)}, bf16[32,128]{1,0:T(8,128)(2,1)S(1)}, u32[]{:S(2)}, u32[]{:S(2)}) collective-permute-start(bf16[32,128]{1,0:T(8,128)(2,1)S(1)} %bitcast.68), channel_id=1, source_target_pairs={{0,24},{8,0},{16,8},{24,16},{1,25},{9,1},{17,9},{25,17},{2,26},{10... | collective-permute-start | bytes 24584 | tf_op jit(solution)/shard_map/ppermute | solution.py:573
  196.1 1.5 collective-permute-done.11
  197.6 3.3 %collective-permute-done.9 = bf16[32,128]{1,0:T(8,128)(2,1)S(1)} collective-permute-done((bf16[32,128]{1,0:T(8,128)(2,1)S(1)}, bf16[32,128]{1,0:T(8,128)(2,1)S(1)}, u32[]{:S(2)}, u32[]{:S(2)}) %collective-permute-start.9) | collective-permute-done | bytes 8224 | tf_op jit(solution)/shard_map/ppermute | solution.py:573
  200.9 1.3 add_convert_fusion
  202.3 2.2 %shard_map.163.rest_0_ = bf16[96,64,256]{2,1,0:T(8,128)(2,1)} custom-call(s32[96]{0:T(128)} %sub.25.spots_ref, bf16[24,64,256]{2,1,0:T(8,128)(2,1)} %bitcast.57, bf16[96,64,256]{2,1,0:T(8,128)(2,1)} %shard_map.162.rest_0_), custom_call_target="tpu_custom_call", output_to_operand_aliasing={{}: (2, {})} | custom-call | tf_op jit(solution)/shard_map/pallas_call | solution.py:120
  204.5 2.2 %shard_map.164.rest_0_ = bf16[96,64,256]{2,1,0:T(8,128)(2,1)} custom-call(s32[96]{0:T(128)} %sub.25.spots_ref, bf16[24,64,256]{2,1,0:T(8,128)(2,1)} %bitcast.58, bf16[96,64,256]{2,1,0:T(8,128)(2,1)} %shard_map.163.rest_0_), custom_call_target="tpu_custom_call", output_to_operand_aliasing={{}: (2, {})} | custom-call | tf_op jit(solution)/shard_map/pallas_call | solution.py:120
  207.6 2.2 %shard_map.165 = bf16[96,64,256]{2,1,0:T(8,128)(2,1)} custom-call(s32[96]{0:T(128)} %sub.25.spots_ref, bf16[24,64,256]{2,1,0:T(8,128)(2,1)} %bitcast.59, bf16[96,64,256]{2,1,0:T(8,128)(2,1)} %shard_map.164.rest_0_), custom_call_target="tpu_custom_call", output_to_operand_aliasing={{}: (2, {})} | custom-call | tf_op jit(solution)/shard_map/pallas_call | solution.py:120
  (91 shorter events, 20.8 us)
Async XLA Ops:
  0.6 2.0 copy-start
  24.6 6.1 %collective-permute-start.3 = (bf16[144,128]{1,0:T(8,128)(2,1)}, bf16[144,128]{1,0:T(8,128)(2,1)S(1)}, u32[]{:S(2)}, u32[]{:S(2)}) collective-permute-start(bf16[144,128]{1,0:T(8,128)(2,1)} %shard_map.167.refs_0_), channel_id=1, source_target_pairs={{0,8},{8,16},{16,24},{24,0},{1,9},{9,17},{17,25},{25,1},{2,10},{10... | collective-permute-start | bytes 110600 | tf_op jit(solution)/shard_map/ppermute | solution.py:540
  26.4 5.3 %collective-permute-start.4 = (bf16[144,128]{1,0:T(8,128)(2,1)}, bf16[144,128]{1,0:T(8,128)(2,1)S(1)}, u32[]{:S(2)}, u32[]{:S(2)}) collective-permute-start(bf16[144,128]{1,0:T(8,128)(2,1)} %shard_map.167.refs_0_), channel_id=1, source_target_pairs={{0,16},{8,24},{16,0},{24,8},{1,17},{9,25},{17,1},{25,9},{2,18},{10... | collective-permute-start | bytes 110600 | tf_op jit(solution)/shard_map/ppermute | solution.py:540
  28.6 4.2 %collective-permute-start.5 = (bf16[144,128]{1,0:T(8,128)(2,1)}, bf16[144,128]{1,0:T(8,128)(2,1)S(1)}, u32[]{:S(2)}, u32[]{:S(2)}) collective-permute-start(bf16[144,128]{1,0:T(8,128)(2,1)} %shard_map.167.refs_0_), channel_id=1, source_target_pairs={{0,24},{8,0},{16,8},{24,16},{1,25},{9,1},{17,9},{25,17},{2,26},{10... | collective-permute-start | bytes 110600 | tf_op jit(solution)/shard_map/ppermute | solution.py:540
  30.7 2.2 %copy-start.11 = (bf16[144,128]{1,0:T(8,128)(2,1)}, bf16[144,128]{1,0:T(8,128)(2,1)S(1)}, u32[]{:S(2)}) copy-start(bf16[144,128]{1,0:T(8,128)(2,1)S(1)} %collective-permute-done.3.refs_1_) | copy-start | bytes 110596
  31.7 1.1 copy-start.12
  32.8 0.6 copy-start.13
  36.5 10.3 %all-to-all-start.5 = ((bf16[8,32,512]{2,1,0:T(8,128)(2,1)}), bf16[8,32,512]{2,1,0:T(8,128)(2,1)S(1)}, u32[]{:S(2)}, u32[]{:S(2)}) async-start(bf16[8,32,512]{2,1,0:T(8,128)(2,1)} %broadcast_in_dim.32), calls=%async_computation.5 | async-start | bytes 524288 | tf_op jit(solution)/shard_map/all_to_all | solution.py:442
  46.8 0.7 copy-start.8
  49.9 5.8 %collective-permute-start.6 = (bf16[64,128]{1,0:T(8,128)(2,1)}, bf16[64,128]{1,0:T(8,128)(2,1)S(1)}, u32[]{:S(2)}, u32[]{:S(2)}) collective-permute-start(bf16[64,128]{1,0:T(8,128)(2,1)} %get-tuple-element.7.refs_0_), channel_id=1, source_target_pairs={{0,8},{8,16},{16,24},{24,0},{1,9},{9,17},{17,25},{25,1},{2,10},{10... | collective-permute-start | bytes 49160 | tf_op jit(solution)/shard_map/ppermute | solution.py:553
  50.4 5.4 %collective-permute-start.7 = (bf16[64,128]{1,0:T(8,128)(2,1)}, bf16[64,128]{1,0:T(8,128)(2,1)S(1)}, u32[]{:S(2)}, u32[]{:S(2)}) collective-permute-start(bf16[64,128]{1,0:T(8,128)(2,1)} %get-tuple-element.7.refs_0_), channel_id=1, source_target_pairs={{0,16},{8,24},{16,0},{24,8},{1,17},{9,25},{17,1},{25,9},{2,18},{10... | collective-permute-start | bytes 49160 | tf_op jit(solution)/shard_map/ppermute | solution.py:553
  53.6 3.9 %collective-permute-start.8 = (bf16[64,128]{1,0:T(8,128)(2,1)}, bf16[64,128]{1,0:T(8,128)(2,1)S(1)}, u32[]{:S(2)}, u32[]{:S(2)}) collective-permute-start(bf16[64,128]{1,0:T(8,128)(2,1)} %get-tuple-element.7.refs_0_), channel_id=1, source_target_pairs={{0,24},{8,0},{16,8},{24,16},{1,25},{9,1},{17,9},{25,17},{2,26},{10... | collective-permute-start | bytes 49160 | tf_op jit(solution)/shard_map/ppermute | solution.py:553
  55.8 1.8 copy-start.14
  55.8 1.8 copy-start.15
  57.6 0.6 copy-start.16
  61.3 13.3 %all-to-all-start.6 = ((bf16[8,5,32,128]{3,2,1,0:T(8,128)(2,1)}), bf16[8,5,32,128]{3,2,1,0:T(8,128)(2,1)S(1)}, u32[]{:S(2)}, u32[]{:S(2)}) async-start(bf16[8,5,32,128]{3,2,1,0:T(8,128)(2,1)} %broadcast_in_dim.33), calls=%async_computation.6 | async-start | bytes 655360 | tf_op jit(solution)/shard_map/all_to_all | solution.py:442
  69.1 45.7 %collective-permute-start.2 = (bf16[8,3,64,256]{3,2,1,0:T(8,128)(2,1)}, bf16[8,3,64,256]{3,2,1,0:T(8,128)(2,1)}, u32[]{:S(2)}, u32[]{:S(2)}) collective-permute-start(bf16[8,3,64,256]{3,2,1,0:T(8,128)(2,1)} %shard_map.160), channel_id=1, source_target_pairs={{0,8},{8,16},{16,24},{24,0},{1,9},{9,17},{17,25},{25,1},{2,10},{10... | collective-permute-start | bytes 2359304 | tf_op jit(solution)/shard_map/ppermute | solution.py:517
  74.6 4.1 %copy-start.7 = (bf16[8,5,32,128]{3,2,1,0:T(8,128)(2,1)}, bf16[8,5,32,128]{3,2,1,0:T(8,128)(2,1)S(1)}, u32[]{:S(2)}) copy-start(bf16[8,5,32,128]{3,2,1,0:T(8,128)(2,1)S(1)} %all-to-all-done.6.all_ref) | copy-start | bytes 983044
  74.6 29.8 %all-to-all-start.3 = ((bf16[8,3,64,256]{3,2,1,0:T(8,128)(2,1)}), bf16[8,3,64,256]{3,2,1,0:T(8,128)(2,1)S(1)}, u32[]{:S(2)}, u32[]{:S(2)}) async-start(bf16[8,3,64,256]{3,2,1,0:T(8,128)(2,1)} %shard_map.161), calls=%async_computation.3 | async-start | bytes 1572864 | tf_op jit(solution)/shard_map/all_to_all | solution.py:580
  80.8 10.7 %copy-start.6 = (bf16[32,4096]{1,0:T(8,128)(2,1)S(1)}, bf16[32,4096]{1,0:T(8,128)(2,1)}, u32[]{:S(2)}) copy-start(bf16[32,4096]{1,0:T(8,128)(2,1)} %get-tuple-element.9) | copy-start | bytes 786436
  82.6 18.0 %slice-start = ((s8[16777216]{0:T(1024)(128)(4,1)}), s8[4194304]{0:T(1024)(128)(4,1)S(1)}, s32[]{:S(2)}) async-start(s8[16777216]{0:T(1024)(128)(4,1)} %bitcast.55), calls=%async_computation.8 | async-start | bytes 8388608
  82.6 18.0 %slice-start.1 = ((s8[16777216]{0:T(1024)(128)(4,1)}), s8[4194304]{0:T(1024)(128)(4,1)S(1)}, s32[]{:S(2)}) async-start(s8[16777216]{0:T(1024)(128)(4,1)} %bitcast.55), calls=%async_computation.9 | async-start | bytes 8388608
  91.6 9.0 %slice-start.2 = ((s8[16777216]{0:T(1024)(128)(4,1)}), s8[4194304]{0:T(1024)(128)(4,1)S(1)}, s32[]{:S(2)}) async-start(s8[16777216]{0:T(1024)(128)(4,1)} %bitcast.55), calls=%async_computation.10 | async-start | bytes 8388608
  91.6 9.0 %slice-start.3 = ((s8[16777216]{0:T(1024)(128)(4,1)}), s8[4194304]{0:T(1024)(128)(4,1)S(1)}, s32[]{:S(2)}) async-start(s8[16777216]{0:T(1024)(128)(4,1)} %bitcast.55), calls=%async_computation.11 | async-start | bytes 8388608
  100.6 55.9 %copy-start.17 = (s32[384]{0:T(512)S(1)}, s32[384]{0:T(512)}, u32[]{:S(2)}) copy-start(s32[384]{0:T(512)} %param.18) | copy-start | bytes 4612
  104.5 69.3 %copy-start.5 = (bf16[8,3,64,256]{3,2,1,0:T(8,128)(2,1)}, bf16[8,3,64,256]{3,2,1,0:T(8,128)(2,1)S(1)}, u32[]{:S(2)}) copy-start(bf16[8,3,64,256]{3,2,1,0:T(8,128)(2,1)S(1)} %all-to-all-done.3) | copy-start | bytes 2359300
  104.5 11.1 %all-to-all-start.7 = ((bf16[8,4,32,128]{3,1,2,0:T(4,128)(2,1)}), bf16[8,4,32,128]{3,1,2,0:T(4,128)(2,1)S(1)}, u32[]{:S(2)}, u32[]{:S(2)}) async-start(bf16[8,4,32,128]{3,1,2,0:T(4,128)(2,1)} %copy.69), calls=%async_computation.7 | async-start | bytes 524288 | tf_op jit(solution)/shard_map/all_to_all | solution.py:567
  112.2 38.4 %collective-permute-start.1 = (bf16[8,3,64,256]{3,2,1,0:T(8,128)(2,1)}, bf16[8,3,64,256]{3,2,1,0:T(8,128)(2,1)S(1)}, u32[]{:S(2)}, u32[]{:S(2)}) collective-permute-start(bf16[8,3,64,256]{3,2,1,0:T(8,128)(2,1)} %shard_map.159), channel_id=1, source_target_pairs={{0,16},{8,24},{16,0},{24,8},{1,17},{9,25},{17,1},{25,9},{2,18},{10... | collective-permute-start | bytes 2359304 | tf_op jit(solution)/shard_map/ppermute | solution.py:517
  115.6 36.0 %all-to-all-start.2 = ((bf16[8,3,64,256]{3,2,1,0:T(8,128)(2,1)}), bf16[8,3,64,256]{3,2,1,0:T(8,128)(2,1)S(1)}, u32[]{:S(2)}, u32[]{:S(2)}) async-start(bf16[8,3,64,256]{3,2,1,0:T(8,128)(2,1)} %collective-permute-done.2), calls=%async_computation.2 | async-start | bytes 1572864 | tf_op jit(solution)/shard_map/all_to_all | solution.py:580
  119.1 90.8 %copy-start.1 = (bf16[2,16,8,256]{3,2,1,0:T(8,128)(2,1)S(1)}, bf16[2,16,8,256]{3,2,1,0:T(8,128)(2,1)}, u32[]{:S(2)}) copy-start(bf16[2,16,8,256]{3,2,1,0:T(8,128)(2,1)} %param.21) | copy-start | bytes 393220
  122.8 37.3 %collective-permute-start = (bf16[8,3,64,256]{3,2,1,0:T(8,128)(2,1)}, bf16[8,3,64,256]{3,2,1,0:T(8,128)(2,1)S(1)}, u32[]{:S(2)}, u32[]{:S(2)}) collective-permute-start(bf16[8,3,64,256]{3,2,1,0:T(8,128)(2,1)} %shard_map.158), channel_id=1, source_target_pairs={{0,24},{8,0},{16,8},{24,16},{1,25},{9,1},{17,9},{25,17},{2,26},{10... | collective-permute-start | bytes 2359304 | tf_op jit(solution)/shard_map/ppermute | solution.py:517
  150.6 0.9 copy-start.10
  151.5 50.7 %copy-start.2 = (bf16[8,3,64,256]{3,2,1,0:T(8,128)(2,1)}, bf16[8,3,64,256]{3,2,1,0:T(8,128)(2,1)S(1)}, u32[]{:S(2)}) copy-start(bf16[8,3,64,256]{3,2,1,0:T(8,128)(2,1)S(1)} %all-to-all-done.2) | copy-start | bytes 2359300
  151.5 16.8 %all-to-all-start.1 = ((bf16[8,3,64,256]{3,2,1,0:T(8,128)(2,1)}), bf16[8,3,64,256]{3,2,1,0:T(8,128)(2,1)S(1)}, u32[]{:S(2)}, u32[]{:S(2)}) async-start(bf16[8,3,64,256]{3,2,1,0:T(8,128)(2,1)} %copy-done.10), calls=%async_computation.1 | async-start | bytes 1572864 | tf_op jit(solution)/shard_map/all_to_all | solution.py:580
  160.1 0.9 copy-start.9
  168.3 36.2 %copy-start.3 = (bf16[8,3,64,256]{3,2,1,0:T(8,128)(2,1)}, bf16[8,3,64,256]{3,2,1,0:T(8,128)(2,1)S(1)}, u32[]{:S(2)}) copy-start(bf16[8,3,64,256]{3,2,1,0:T(8,128)(2,1)S(1)} %all-to-all-done.1) | copy-start | bytes 2359300
  168.3 38.5 %all-to-all-start = ((bf16[8,3,64,256]{3,2,1,0:T(8,128)(2,1)}), bf16[8,3,64,256]{3,2,1,0:T(8,128)(2,1)S(1)}, u32[]{:S(2)}, u32[]{:S(2)}) async-start(bf16[8,3,64,256]{3,2,1,0:T(8,128)(2,1)} %copy-done.9), calls=%async_computation | async-start | bytes 1572864 | tf_op jit(solution)/shard_map/all_to_all | solution.py:580
  176.2 19.8 %collective-permute-start.10 = (bf16[32,128]{1,0:T(8,128)(2,1)S(1)}, bf16[32,128]{1,0:T(8,128)(2,1)S(1)}, u32[]{:S(2)}, u32[]{:S(2)}) collective-permute-start(bf16[32,128]{1,0:T(8,128)(2,1)S(1)} %bitcast.67), channel_id=1, source_target_pairs={{0,16},{8,24},{16,0},{24,8},{1,17},{9,25},{17,1},{25,9},{2,18},{10... | collective-permute-start | bytes 24584 | tf_op jit(solution)/shard_map/ppermute | solution.py:573
  176.3 21.3 %collective-permute-start.11 = (bf16[32,128]{1,0:T(8,128)(2,1)S(1)}, bf16[32,128]{1,0:T(8,128)(2,1)S(1)}, u32[]{:S(2)}, u32[]{:S(2)}) collective-permute-start(bf16[32,128]{1,0:T(8,128)(2,1)S(1)} %bitcast.68), channel_id=1, source_target_pairs={{0,24},{8,0},{16,8},{24,16},{1,25},{9,1},{17,9},{25,17},{2,26},{10... | collective-permute-start | bytes 24584 | tf_op jit(solution)/shard_map/ppermute | solution.py:573
  195.5 5.4 %collective-permute-start.9 = (bf16[32,128]{1,0:T(8,128)(2,1)S(1)}, bf16[32,128]{1,0:T(8,128)(2,1)S(1)}, u32[]{:S(2)}, u32[]{:S(2)}) collective-permute-start(bf16[32,128]{1,0:T(8,128)(2,1)S(1)} %bitcast.69), channel_id=1, source_target_pairs={{0,8},{8,16},{16,24},{24,0},{1,9},{9,17},{17,25},{25,1},{2,10},{10... | collective-permute-start | bytes 24584 | tf_op jit(solution)/shard_map/ppermute | solution.py:573
  206.8 0.9 copy-start.4
